TPU v7x, 256 devices: a whole 4x4x8 slice. The times are simulated.
256 devices in a mesh: req: 32 (over z_hi, x, y), tp: 8 (over z_lo, core).
Axes of the slice: x: 4, y: 4, z: 8 (z_hi: 2, z_lo: 4; z = z_hi * 4 + z_lo), core: 2. Of those that a mesh axis runs over, the one named last changes fastest.
Arguments:
- hidden: bfloat16 [4096, 2048], P('req', 'tp'), may hold values from -6 to 6
- attn_gain: bfloat16 [2048], replicated, may hold values from 0.099609375 to 1.8984375
- w_qkv: bfloat16 [3, 2048, 2048], P(None, None, 'tp'), may hold values from -0.125 to 0.125
- w_out: bfloat16 [2048, 2048], P('tp'), may hold values from -0.125 to 0.125
- kv_cache: bfloat16 [2, 32, 1024, 2048], P(None, 'req', None, 'tp'), as said below
- holder_slot: int32 [32], replicated, may hold values from 0 to 31, as said below
- lengths: int32 [32], P('req'), may hold values from 1 to 1024, as said below
- ffn_gain: bfloat16 [2048], replicated, may hold values from 0.099609375 to 1.8984375
- w_router: bfloat16 [2048, 32], replicated
- expert_ids: int32 [4096, 6], P('req'), may hold values from 0 to 31, all different within a row; in each aligned block of 128 rows (0 to 127, 128 to 255, ...) at most 32 rows name the same one
- w_exp_in: bfloat16 [32, 2, 2048, 1408], P('req', None, None, 'tp'), may hold values from -0.4375 to 0.4375
- w_exp_down: bfloat16 [32, 1408, 2048], P('req', 'tp'), may hold values from -0.5 to 0.5
- w_sh_in: bfloat16 [2, 2048, 1408], P(None, None, 'tp'), may hold values from -0.125 to 0.125
- w_sh_down: bfloat16 [1408, 2048], P('tp'), may hold values from -0.15625 to 0.15625
- final_gain: bfloat16 [2048], replicated, may hold values from 0.5 to 1.5
- w_head: bfloat16 [51200, 2048], P(('req', 'tp')), may hold values from -0.5 to 0.5
Outputs:
- out_hidden: bfloat16 [4096, 2048], P('req', 'tp')
- new_cache: bfloat16 [2, 32, 128, 2048], P(None, 'req', None, 'tp')
- last_rms: float32 [32], replicated
- top_logit: float32 [32], replicated
Inputs may be any that keep to these rules, and one draw needn't show every extreme that they name: `kv_cache`: the cache in slot s lies on index s // 1 of req; request r is owned by index r. `holder_slot`: A permutation of the cache slots; about half of the requests keep their own slot. `lengths`: some request has exactly 1024 cached positions. `expert_ids`: within the rows of one device (128 aligned tokens) each expert is named by at most 32 rows, a bound that is reached.
All inputs are finite; a program needn't handle non-finite values.
Results may differ from a plain program's by a relative error of at most 0.025.
Values may be sent and summed in bfloat16 or wider, within the bound.
No kernel may reach another device: no remote copies, remote signals or barrier semaphores. Data moves between devices by JAX's collectives and lax.ppermute only.
A program may use at most 64 MiB of HBM per device.

v0:
```python
import jax
import jax.numpy as jnp
from jax import lax
from jax.sharding import PartitionSpec as P

HD = 128
TOPK = 6
CAP = 32
epsilon = 1e-06


def rms_scale(values, gain):
    return (
        values
        * lax.rsqrt(jnp.mean(values * values, axis=-1, keepdims=True) + epsilon)
        * gain.astype(jnp.float32)
    )


def rotate_half(values, positions):
    half_len = values.shape[-1] // 2
    freqs = 10000.0 ** (-2.0 * jnp.arange(half_len, dtype=jnp.float32) / values.shape[-1])
    angles = positions[..., None] * freqs
    cosine = jnp.cos(angles)[..., None, :]
    sine = jnp.sin(angles)[..., None, :]
    lead_half = values[..., :half_len]
    tail_half = values[..., half_len:]
    return jnp.concatenate(
        [lead_half * cosine - tail_half * sine, tail_half * cosine + lead_half * sine], axis=-1
    )


def attend(queries, keys_new, values_new, old_keys, old_values, lengths):
    context_len = old_keys.shape[1]
    new_len = queries.shape[1]
    all_keys = jnp.concatenate([old_keys, keys_new], axis=1)
    all_values = jnp.concatenate([old_values, values_new], axis=1)
    scores = jnp.einsum(
        "rthd,rshd->rhts", queries, all_keys, preferred_element_type=jnp.float32
    ) * queries.shape[-1] ** (-0.5)
    column = jnp.arange(context_len + new_len)[None, None, :]
    row_pos = jnp.arange(new_len)[None, :, None]
    visible = jnp.where(
        column < context_len, column < lengths[:, None, None], column - context_len <= row_pos
    )
    visible = visible[:, None]
    masked = jnp.where(visible, scores, -1e30)
    peak = jnp.max(masked, axis=-1, keepdims=True)
    raised = jnp.where(visible, jnp.exp(masked - peak), 0.0)
    weights = (raised / jnp.sum(raised, axis=-1, keepdims=True)).astype(jnp.bfloat16)
    mixed = jnp.einsum("rhts,rshd->rthd", weights, all_values, preferred_element_type=jnp.float32)
    return mixed.astype(jnp.bfloat16)


def expert_block(arrived, w_exp_in, w_exp_down):
    both = jnp.einsum("nekd,ecdf->cnekf", arrived, w_exp_in, preferred_element_type=jnp.float32)
    inner = (jax.nn.silu(both[0]) * both[1]).astype(jnp.bfloat16)
    return jnp.einsum(
        "nekf,efd->nekd", inner, w_exp_down, preferred_element_type=jnp.float32
    ).astype(jnp.bfloat16)


def local(
    hidden,
    attn_gain,
    w_qkv,
    w_out,
    kv_cache,
    holder_slot,
    lengths,
    ffn_gain,
    w_router,
    expert_ids,
    w_exp_in,
    w_exp_down,
    w_sh_in,
    w_sh_down,
    final_gain,
    w_head,
):
    req_size = lax.axis_size("req")
    tp_pos = lax.axis_index("tp")
    full_in = lax.all_gather(hidden, "tp", axis=1, tiled=True)
    tok_rows = full_in.shape[0]
    slot_count = kv_cache.shape[1]
    new_len = tok_rows // slot_count
    local_feat = hidden.shape[1]
    local_heads = w_qkv.shape[2] // HD
    normed = rms_scale(full_in.astype(jnp.float32), attn_gain).astype(jnp.bfloat16)
    projected = jnp.einsum("td,cde->cte", normed, w_qkv, preferred_element_type=jnp.float32)
    positions = (lengths[:, None] + jnp.arange(new_len, dtype=jnp.int32)[None, :]).astype(
        jnp.float32
    )
    shaped = projected.reshape(3, slot_count, new_len, local_heads, HD)
    queries = rotate_half(shaped[0], positions).astype(jnp.bfloat16)
    keys_new = rotate_half(shaped[1], positions).astype(jnp.bfloat16)
    values_new = shaped[2].astype(jnp.bfloat16)
    new_cache = jnp.stack([keys_new, values_new]).reshape(2, slot_count, new_len, local_heads * HD)
    spread = lax.all_to_all(kv_cache, "req", split_axis=2, concat_axis=1, tiled=True)
    ordered = jnp.take(spread, holder_slot, axis=1)
    fetched = lax.all_to_all(ordered, "req", split_axis=1, concat_axis=2, tiled=True)
    context_len = fetched.shape[2]
    old_pair = fetched.reshape(2, slot_count, context_len, local_heads, HD)
    attn_out = attend(queries, keys_new, values_new, old_pair[0], old_pair[1], lengths)
    attn_out = attn_out.reshape(tok_rows, local_heads * HD)
    attn_total = lax.psum(
        jnp.dot(attn_out, w_out, preferred_element_type=jnp.float32).astype(jnp.bfloat16), "tp"
    ).astype(jnp.float32)
    resid = (full_in.astype(jnp.float32) + attn_total).astype(jnp.bfloat16)
    ffn_in = rms_scale(resid.astype(jnp.float32), ffn_gain).astype(jnp.bfloat16)
    probs = jax.nn.softmax(jnp.dot(ffn_in, w_router, preferred_element_type=jnp.float32), axis=-1)
    experts_all = w_router.shape[1]
    expert_local = w_exp_in.shape[0]
    expert_iota = jnp.arange(experts_all, dtype=jnp.int32)
    gates = jnp.sum(
        probs[:, None, :]
        * (expert_ids[:, :, None] == expert_iota[None, None, :]).astype(jnp.float32),
        axis=-1,
    )
    picks = expert_ids.reshape(-1)
    pick_count = picks.shape[0]
    onehot = (picks[:, None] == expert_iota[None, :]).astype(jnp.int32)
    earlier = jnp.cumsum(onehot, axis=0) - onehot
    rank = jnp.sum(earlier * onehot, axis=1)
    slot_of_pick = picks * CAP + rank
    source = (
        jnp.full((experts_all * CAP,), tok_rows, jnp.int32)
        .at[slot_of_pick]
        .set(jnp.arange(pick_count, dtype=jnp.int32) // TOPK)
    )
    padded = jnp.concatenate([ffn_in, jnp.zeros((1, ffn_in.shape[1]), jnp.bfloat16)], axis=0)
    outgoing = jnp.take(padded, source, axis=0).reshape(
        req_size, expert_local, CAP, padded.shape[1]
    )
    served = expert_block(
        lax.all_to_all(outgoing, "req", split_axis=0, concat_axis=0, tiled=True),
        w_exp_in,
        w_exp_down,
    )
    shared_both = jnp.einsum("td,cdf->ctf", ffn_in, w_sh_in, preferred_element_type=jnp.float32)
    shared_inner = (jax.nn.silu(shared_both[0]) * shared_both[1]).astype(jnp.bfloat16)
    shared_terms = jnp.dot(shared_inner, w_sh_down, preferred_element_type=jnp.float32)
    pick_slots = slot_of_pick.reshape(tok_rows, TOPK)
    returned = lax.all_to_all(served, "req", split_axis=0, concat_axis=0, tiled=True)
    returned = returned.reshape(experts_all * CAP, returned.shape[3])
    to_reduce = shared_terms
    for pick_pos in range(TOPK):
        chosen_rows = jnp.take(returned, pick_slots[:, pick_pos], axis=0).astype(jnp.float32)
        to_reduce = to_reduce + chosen_rows * gates[:, pick_pos : pick_pos + 1]
    layer_share = lax.psum_scatter(
        to_reduce.astype(jnp.bfloat16), "tp", scatter_dimension=1, tiled=True
    ).astype(jnp.float32)
    resid_share = lax.dynamic_slice_in_dim(resid, tp_pos * local_feat, local_feat, 1)
    out_hidden = (resid_share.astype(jnp.float32) + layer_share).astype(jnp.bfloat16)
    last_share = out_hidden.reshape(slot_count, new_len, local_feat)[:, new_len - 1]
    last_rows = lax.all_gather(last_share, "tp", axis=1, tiled=True)
    last_every = lax.all_gather(last_rows, "req", axis=0, tiled=True)
    last_tok = last_every.astype(jnp.float32)
    last_rms = jnp.sqrt(jnp.mean(last_tok * last_tok, axis=-1) + epsilon)
    head_in = (last_tok / last_rms[:, None] * final_gain.astype(jnp.float32)).astype(jnp.bfloat16)
    logits = lax.dot_general(
        head_in, w_head, (((1,), (1,)), ((), ())), preferred_element_type=jnp.float32
    )
    top_logit = lax.pmax(jnp.max(logits, axis=1), ("req", "tp"))
    return (out_hidden, new_cache, last_rms, top_logit)


def solution(mesh):
    return jax.shard_map(
        local,
        mesh=mesh,
        in_specs=(
            P("req", "tp"),
            P(),
            P(None, None, "tp"),
            P("tp", None),
            P(None, "req", None, "tp"),
            P(),
            P("req"),
            P(),
            P(),
            P("req", None),
            P("req", None, None, "tp"),
            P("req", "tp", None),
            P(None, None, "tp"),
            P("tp", None),
            P(),
            P(("req", "tp"), None),
        ),
        out_specs=(P("req", "tp"), P(None, "req", None, "tp"), P(), P()),
        check_vma=False,
    )
```

profile of v0, /device:TPU:1, one launch (start us, length us, event | category | flops | bytes accessed | tf_op | source)
XLA Modules:
  0.0 697.8 jit_solution(8037834648569727721)
XLA Ops:
  7.2 3.5 copy.92
  10.7 14.8 %all-to-all-start = ((bf16[2,1,1024,256]{3,0,1,2:T(2,128)(2,1)}), bf16[2,1,1024,256]{3,0,1,2:T(2,128)(2,1)}, u32[]{:S(2)}, u32[]{:S(2)}) async-start(bf16[2,1,1024,256]{3,0,1,2:T(2,128)(2,1)} %copy.92), calls=%async_computation | async-start | bytes 2097152 | tf_op jit(solution)/shard_map/all_to_all | solution.py:99
  28.2 32.7 %all_gather.9 = bf16[128,2048]{1,0:T(8,128)(2,1)S(1)} all-gather(bf16[128,256]{1,0:T(8,128)(2,1)S(1)} %copy-done.8), channel_id=1, replica_groups=mesh['req'=32,'tp'=8] {'tp'}, dimensions={1}, use_global_device_ids=true | all-gather | bytes 589824 | tf_op jit(solution)/shard_map/all_gather | solution.py:83
  70.7 11.3 %all-to-all-start.1 = ((bf16[2,32,32,256]{3,2,0,1:T(8,128)(2,1)}), bf16[2,32,32,256]{3,2,0,1:T(8,128)(2,1)}, u32[]{:S(2)}, u32[]{:S(2)}) async-start(bf16[2,32,32,256]{3,2,0,1:T(8,128)(2,1)} %select_bitcast_fusion), calls=%async_computation.1 | async-start | bytes 2097152 | tf_op jit(solution)/shard_map/all_to_all | solution.py:101
  89.8 15.1 %all-to-all-done.1 = bf16[2,32,32,256]{3,2,0,1:T(8,128)(2,1)} async-done(((bf16[2,32,32,256]{3,2,0,1:T(8,128)(2,1)}), bf16[2,32,32,256]{3,2,0,1:T(8,128)(2,1)}, u32[]{:S(2)}, u32[]{:S(2)}) %all-to-all-start.1) | async-done | bytes 1048608 | tf_op jit(solution)/shard_map/all_to_all | solution.py:101
  115.1 3.3 fusion.79
  121.6 3.5 scatter_custom_fusion
  125.2 67.9 %all-reduce.3.cloned.1.call-done = bf16[128,2048]{1,0:T(8,128)(2,1)} async-done(((bf16[128,2048]{1,0:T(8,128)(2,1)}), bf16[128,2048]{1,0:T(8,128)(2,1)}) %all-reduce.3.cloned.1.call-update) | async-done | bytes 524304 | tf_op jit(solution)/shard_map/psum | solution.py:106
  197.4 10.0 %gather_fusion.1 = bf16[1024,2048]{1,0:T(8,128)(2,1)} fusion(bf16[129,2048]{1,0:T(8,128)(2,1)} %concatenate.47, s32[1024]{0:T(1024)S(1)} %fusion.61), kind=kCustom, calls=%fused_computation.7 | custom fusion | bytes 8392704 | tf_op jit(solution)/shard_map/jit(_take)/gather | solution.py:132
  210.0 106.0 %all_to_all.31 = bf16[32,1,32,2048]{3,2,1,0:T(8,128)(2,1)S(1)} all-to-all(bf16[32,1,32,2048]{3,2,1,0:T(8,128)(2,1)S(1)} %broadcast_select_fusion), channel_id=1, replica_groups=mesh['req'=32,'tp'=8] {'req'}, dimensions={0} | all-to-all | bytes 8388608 | tf_op jit(solution)/shard_map/all_to_all | solution.py:136
  318.4 3.3 convert_bitcast_fusion
  321.7 6.9 all-to-all-start.3
  332.5 81.5 %all-to-all-done.3 = bf16[32,1,32,2048]{3,2,1,0:T(8,128)(2,1)} async-done(((bf16[32,1,32,2048]{3,2,1,0:T(8,128)(2,1)}), bf16[32,1,32,2048]{3,2,1,0:T(8,128)(2,1)}, u32[]{:S(2)}, u32[]{:S(2)}) %all-to-all-start.3) | async-done | bytes 4194336 | tf_op jit(solution)/shard_map/all_to_all | solution.py:144
  413.9 5.0 gather_fusion.7
  418.9 5.0 gather_fusion.6
  423.9 5.0 gather_fusion.5
  428.9 5.0 gather_fusion.4
  433.8 5.0 gather_fusion.3
  438.8 5.0 gather_fusion.2
  443.8 4.0 fusion.12
  448.9 39.4 %reduce-scatter.2.cloned.1.call-done = bf16[128,256]{1,0:T(8,128)(2,1)} async-done(((bf16[128,2048]{1,0:T(8,128)(2,1)}), bf16[128,256]{1,0:T(8,128)(2,1)}) %reduce-scatter.2.cloned.1.call-update) | async-done | bytes 65552 | tf_op jit(solution)/shard_map/reduce_scatter | solution.py:150
  489.2 12.1 %all-gather = bf16[1,1,2048]{2,1,0:T(2,128)(2,1)S(1)} all-gather(bf16[1,1,256]{2,1,0:T(2,128)(2,1)S(1)} %slice.154), channel_id=2, replica_groups=mesh['req'=32,'tp'=8] {'tp'}, dimensions={2}, use_global_device_ids=true | all-gather | bytes 4608 | tf_op jit(solution)/shard_map/all_gather | solution.py:156
  501.3 101.8 %all-gather.1 = bf16[32,1,2048]{2,1,0:T(2,128)(2,1)S(1)} all-gather(bf16[1,1,2048]{2,1,0:T(2,128)(2,1)S(1)} %all-gather), channel_id=3, replica_groups=mesh['req'=32,'tp'=8] {'req'}, dimensions={0}, use_global_device_ids=true | all-gather | bytes 135168 | tf_op jit(solution)/shard_map/all_gather | solution.py:157
  605.9 85.0 %pmax.7 = f32[32]{0:T(128)} all-reduce(f32[32]{0:T(128)S(1)} %convolution_reduce_fusion), channel_id=1, replica_groups=mesh['req'=32,'tp'=8] {'req','tp'}, use_global_device_ids=true, to_apply=%region_15.17 | all-reduce | flops 32 | bytes 256 | tf_op jit(solution)/shard_map/pmax | solution.py:164
  (125 shorter events, 50.7 us)
Async XLA Ops:
  7.2 54.5 %copy-start = (bf16[3,2048,256]{2,1,0:T(8,128)(2,1)S(1)}, bf16[3,2048,256]{2,1,0:T(8,128)(2,1)}, u32[]{:S(2)}) copy-start(bf16[3,2048,256]{2,1,0:T(8,128)(2,1)} %param.20) | copy-start | bytes 9437188
  10.7 14.8 %copy-start.10 = (s32[128,6]{0,1:T(8,128)S(1)}, s32[128,6]{0,1:T(8,128)}, u32[]{:S(2)}) copy-start(s32[128,6]{0,1:T(8,128)} %param.27) | copy-start | bytes 9220
  10.7 15.2 %copy-start.12 = (bf16[2048]{0:T(1024)(128)(2,1)S(1)}, bf16[2048]{0:T(1024)(128)(2,1)}, u32[]{:S(2)}) copy-start(bf16[2048]{0:T(1024)(128)(2,1)} %param.19) | copy-start | bytes 12292
  10.7 17.5 %copy-start.17 = (s32[32]{0:T(128)S(1)}, s32[32]{0:T(128)}, u32[]{:S(2)}) copy-start(s32[32]{0:T(128)} %param.23) | copy-start | bytes 388
  10.7 17.5 %copy-start.8 = (bf16[128,256]{1,0:T(8,128)(2,1)S(1)}, bf16[128,256]{1,0:T(8,128)(2,1)}, u32[]{:S(2)}) copy-start(bf16[128,256]{1,0:T(8,128)(2,1)} %param.18) | copy-start | bytes 196612
  10.7 52.4 %all-to-all-start = ((bf16[2,1,1024,256]{3,0,1,2:T(2,128)(2,1)}), bf16[2,1,1024,256]{3,0,1,2:T(2,128)(2,1)}, u32[]{:S(2)}, u32[]{:S(2)}) async-start(bf16[2,1,1024,256]{3,0,1,2:T(2,128)(2,1)} %copy.92), calls=%async_computation | async-start | bytes 2097152 | tf_op jit(solution)/shard_map/all_to_all | solution.py:99
  60.9 0.8 copy-start.1
  70.7 12.0 %copy-start.13 = (bf16[2048]{0:T(1024)(128)(2,1)S(1)}, bf16[2048]{0:T(1024)(128)(2,1)}, u32[]{:S(2)}) copy-start(bf16[2048]{0:T(1024)(128)(2,1)} %param.25) | copy-start | bytes 12292
  70.7 34.3 %all-to-all-start.1 = ((bf16[2,32,32,256]{3,2,0,1:T(8,128)(2,1)}), bf16[2,32,32,256]{3,2,0,1:T(8,128)(2,1)}, u32[]{:S(2)}, u32[]{:S(2)}) async-start(bf16[2,32,32,256]{3,2,0,1:T(8,128)(2,1)} %select_bitcast_fusion), calls=%async_computation.1 | async-start | bytes 2097152 | tf_op jit(solution)/shard_map/all_to_all | solution.py:101
  81.9 111.3 %all-reduce.3.cloned.1.call-start = ((), (), s32[]{:S(2)}) async-start(), calls=%async_computation.5 | async-start | bytes 1048576 | tf_op jit(solution)/shard_map/psum | solution.py:106
  118.5 2.0 copy-start.5
  121.6 73.9 %copy-start.9 = (f32[2048]{0:T(1024)S(1)}, f32[2048]{0:T(1024)}, u32[]{:S(2)}) copy-start(f32[2048]{0:T(1024)} %convert_element_type.185) | copy-start | bytes 24580
  194.6 0.8 copy-start.4
  195.7 0.9 copy-start.2
  210.0 106.0 %copy-start.15 = (bf16[1,2,2048,176]{2,3,1,0:T(8,128)(2,1)S(1)}, bf16[1,2,2048,176]{2,3,1,0:T(8,128)(2,1)}, u32[]{:S(2)}) copy-start(bf16[1,2,2048,176]{2,3,1,0:T(8,128)(2,1)} %param.28) | copy-start | bytes 4325380
  316.0 2.3 copy-start.16
  321.7 7.4 %copy-start.6 = (bf16[2048,32]{0,1:T(8,128)(2,1)S(1)}, bf16[2048,32]{0,1:T(8,128)(2,1)}, u32[]{:S(2)}) copy-start(bf16[2048,32]{0,1:T(8,128)(2,1)} %param.26) | copy-start | bytes 393220
  321.7 8.8 %copy-start.11 = (s32[128,6]{0,1:T(8,128)S(1)}, s32[128,6]{0,1:T(8,128)}, u32[]{:S(2)}) copy-start(s32[128,6]{0,1:T(8,128)} %param.27) | copy-start | bytes 9220
  321.7 92.3 %all-to-all-start.3 = ((bf16[32,1,32,2048]{3,2,1,0:T(8,128)(2,1)}), bf16[32,1,32,2048]{3,2,1,0:T(8,128)(2,1)}, u32[]{:S(2)}, u32[]{:S(2)}) async-start(bf16[32,1,32,2048]{3,2,1,0:T(8,128)(2,1)} %convert_bitcast_fusion), calls=%async_computation.3 | async-start | bytes 8388608 | tf_op jit(solution)/shard_map/all_to_all | solution.py:144
  328.6 159.7 %reduce-scatter.2.cloned.1.call-start = ((), (), s32[]{:S(2)}) async-start(), calls=%async_computation.6 | async-start | bytes 589824 | tf_op jit(solution)/shard_map/reduce_scatter | solution.py:150
  328.6 1.9 copy-start.3
  443.8 4.1 copy-start.14
  489.2 116.8 %copy-start.7 = (bf16[128,256]{1,0:T(8,128)(2,1)}, bf16[128,256]{1,0:T(8,128)(2,1)S(1)}, u32[]{:S(2)}) copy-start(bf16[128,256]{1,0:T(8,128)(2,1)S(1)} %add_convert_fusion) | copy-start | bytes 196612
  603.6 87.3 %copy-start.18 = (f32[32]{0:T(128)}, f32[32]{0:T(128)S(1)}, u32[]{:S(2)}) copy-start(f32[32]{0:T(128)S(1)} %add_sqrt_fusion) | copy-start | bytes 388
Sparse Core Ops, SparseCore 0:
  121.7 71.4 all-reduce.2
  448.0 40.2 reduce-scatter.1
where the time goes:
time: 699 us; the launch traced here: 698 us
  blocking collectives  338 us (48%)
  waiting for transfers between devices  204 us (29%)
  local copies, waits for them, and re-layouts  72.3 us (10%)
  starting transfers between devices  33 us (5%)
  matrix products  22.3 us (3%)
  between operations  15.2 us (2%)
  other arithmetic  13.4 us (2%)
    all_to_all x1, blocking collectives, local(): lax.all_to_all(outgoing, 'req', split_axis=0, concat_axis=0, tiled=True)  106 us
    all_gather x1, blocking collectives, local(): last_every = lax.all_gather(last_rows, 'req', axis=0, tiled=True)  102 us
    pmax x1, blocking collectives, local(): top_logit = lax.pmax(jnp.max(logits, axis=1), ('req', 'tp'))  85 us
    all_to_all x1, waiting for transfers between devices, local(): lax.all_to_all(served, 'req', split_axis=0, concat_axis=0, tiled=True)  81.5 us
    psum x1, waiting for transfers between devices, local(): lax.psum(jnp.dot(attn_out, w_out, preferred_element_type=jnp.float32).ast...  67.9 us
    reduce_scatter x1, waiting for transfers between devices, local(): lax.psum_scatter(to_reduce.astype(jnp.bfloat16), 'tp', scatter_dimension=...  39.4 us
    all_gather x1, blocking collectives, local(): full_in = lax.all_gather(hidden, 'tp', axis=1, tiled=True)  32.7 us
    gather x6, local copies, waits for them, and re-layouts, local(): jnp.take(returned, pick_slots[:, pick_pos], axis=0).astype(jnp.float32)  29.9 us
  transfers between devices with their start and end apart: 5, of which 4 were waited for; matrix products, arithmetic and copies ran while one was open for 3% of the time, Pallas kernels for 0%

commit v1 on v0

--- a/solution.py
+++ b/solution.py
@@ -80,7 +80,9 @@
 ):
     req_size = lax.axis_size("req")
     tp_pos = lax.axis_index("tp")
-    full_in = lax.all_gather(hidden, "tp", axis=1, tiled=True)
+    full_in = jnp.concatenate(
+        lax.all_to_all(jnp.stack([hidden] * lax.axis_size("tp")), "tp", 0, 0), axis=1
+    )
     tok_rows = full_in.shape[0]
     slot_count = kv_cache.shape[1]
     new_len = tok_rows // slot_count

time: 699 us -> 698 us (level)
  blocking collectives: 338 us -> 305 us
  waiting for transfers between devices: 204 us -> 224 us
  starting transfers between devices: 33 us -> 40.4 us
    all_gather x1 -> x0, blocking collectives: 32.7 us -> none  [local(): full_in = lax.all_gather(hidden, 'tp', axis=1, tiled=True)]
    all_to_all x1, waiting for transfers between devices: 0.01 us -> 16.2 us  [local(): lax.all_to_all(kv_cache, 'req', split_axis=2, concat_axis=1, tiled=True)]
    all_to_all x0 -> x1, starting transfers between devices: none -> 14 us  [local(): lax.all_to_all(jnp.stack([hidden] * lax.axis_size('tp')), 'tp', 0, 0)]
  transfers between devices with their start and end apart: 5 -> 6, of which waited for: 4 -> 6; matrix products, arithmetic and copies ran while one was open for 3% -> 4% of each run, Pallas kernels for 0% -> 0%
where the time goes in v1:
time: 698 us; the launch traced here: 697 us
  blocking collectives  305 us (44%)
  waiting for transfers between devices  224 us (32%)
  local copies, waits for them, and re-layouts  72.3 us (10%)
  starting transfers between devices  40.4 us (6%)
  matrix products  21.6 us (3%)
  other arithmetic  18.2 us (3%)
  between operations  15.3 us (2%)
    all_to_all x1, blocking collectives, local(): lax.all_to_all(outgoing, 'req', split_axis=0, concat_axis=0, tiled=True)  106 us
    all_gather x1, blocking collectives, local(): last_every = lax.all_gather(last_rows, 'req', axis=0, tiled=True)  102 us
    pmax x1, blocking collectives, local(): top_logit = lax.pmax(jnp.max(logits, axis=1), ('req', 'tp'))  84.9 us
    all_to_all x1, waiting for transfers between devices, local(): lax.all_to_all(served, 'req', split_axis=0, concat_axis=0, tiled=True)  81.4 us
    psum x1, waiting for transfers between devices, local(): lax.psum(jnp.dot(attn_out, w_out, preferred_element_type=jnp.float32).ast...  64 us
    reduce_scatter x1, waiting for transfers between devices, local(): lax.psum_scatter(to_reduce.astype(jnp.bfloat16), 'tp', scatter_dimension=...  39.4 us
    gather x6, local copies, waits for them, and re-layouts, local(): jnp.take(returned, pick_slots[:, pick_pos], axis=0).astype(jnp.float32)  29.9 us
    all_to_all x1, waiting for transfers between devices, local(): lax.all_to_all(ordered, 'req', split_axis=1, concat_axis=2, tiled=True)  16.5 us
  transfers between devices with their start and end apart: 6, of which 6 were waited for; matrix products, arithmetic and copies ran while one was open for 4% of the time, Pallas kernels for 0%

profile of v1, /device:TPU:1, one launch (start us, length us, event | category | flops | bytes accessed | tf_op | source)
XLA Modules:
  0.0 696.6 jit_solution(441520342853747126)
XLA Ops:
  7.2 3.5 copy.95
  10.7 14.8 %all-to-all-start.1 = ((bf16[2,1,1024,256]{3,0,1,2:T(2,128)(2,1)}), bf16[2,1,1024,256]{3,0,1,2:T(2,128)(2,1)}, u32[]{:S(2)}, u32[]{:S(2)}) async-start(bf16[2,1,1024,256]{3,0,1,2:T(2,128)(2,1)} %copy.95), calls=%async_computation.1 | async-start | bytes 2097152 | tf_op jit(solution)/shard_map/all_to_all | solution.py:101
  30.3 16.2 %all-to-all-done.1 = bf16[2,1,1024,256]{3,0,1,2:T(2,128)(2,1)} async-done(((bf16[2,1,1024,256]{3,0,1,2:T(2,128)(2,1)}), bf16[2,1,1024,256]{3,0,1,2:T(2,128)(2,1)}, u32[]{:S(2)}, u32[]{:S(2)}) %all-to-all-start.1) | async-done | bytes 1048608 | tf_op jit(solution)/shard_map/all_to_all | solution.py:101
  47.3 14.0 %all-to-all-start = ((bf16[8,128,256]{2,1,0:T(8,128)(2,1)}), bf16[8,128,256]{2,1,0:T(8,128)(2,1)}, u32[]{:S(2)}, u32[]{:S(2)}) async-start(bf16[8,128,256]{2,1,0:T(8,128)(2,1)} %stack.4), calls=%async_computation | async-start | bytes 1048576 | tf_op jit(solution)/shard_map/all_to_all | solution.py:84
  69.7 6.2 all-to-all-done
  76.0 4.7 all-to-all-start.2
  91.1 16.5 %all-to-all-done.2 = bf16[2,32,32,256]{3,2,0,1:T(8,128)(2,1)} async-done(((bf16[2,32,32,256]{3,2,0,1:T(8,128)(2,1)}), bf16[2,32,32,256]{3,2,0,1:T(8,128)(2,1)}, u32[]{:S(2)}, u32[]{:S(2)}) %all-to-all-start.2) | async-done | bytes 1048608 | tf_op jit(solution)/shard_map/all_to_all | solution.py:103
  124.4 3.5 scatter_custom_fusion
  128.0 64.0 %all-reduce.3.cloned.1.call-done = bf16[128,2048]{1,0:T(8,128)(2,1)} async-done(((bf16[128,2048]{1,0:T(8,128)(2,1)}), bf16[128,2048]{1,0:T(8,128)(2,1)}) %all-reduce.3.cloned.1.call-update) | async-done | bytes 524304 | tf_op jit(solution)/shard_map/psum | solution.py:108
  196.3 10.0 %gather_fusion.1 = bf16[1024,2048]{1,0:T(8,128)(2,1)} fusion(bf16[129,2048]{1,0:T(8,128)(2,1)} %concatenate.47, s32[1024]{0:T(1024)S(1)} %fusion.58), kind=kCustom, calls=%fused_computation.7 | custom fusion | bytes 8392704 | tf_op jit(solution)/shard_map/jit(_take)/gather | solution.py:134
  208.9 106.0 %all_to_all.36 = bf16[32,1,32,2048]{3,2,1,0:T(8,128)(2,1)S(1)} all-to-all(bf16[32,1,32,2048]{3,2,1,0:T(8,128)(2,1)S(1)} %broadcast_select_fusion), channel_id=1, replica_groups=mesh['req'=32,'tp'=8] {'req'}, dimensions={0} | all-to-all | bytes 8388608 | tf_op jit(solution)/shard_map/all_to_all | solution.py:138
  320.6 6.9 all-to-all-start.4
  331.4 81.4 %all-to-all-done.4 = bf16[32,1,32,2048]{3,2,1,0:T(8,128)(2,1)} async-done(((bf16[32,1,32,2048]{3,2,1,0:T(8,128)(2,1)}), bf16[32,1,32,2048]{3,2,1,0:T(8,128)(2,1)}, u32[]{:S(2)}, u32[]{:S(2)}) %all-to-all-start.4) | async-done | bytes 4194336 | tf_op jit(solution)/shard_map/all_to_all | solution.py:146
  412.8 5.0 gather_fusion.7
  417.8 5.0 gather_fusion.6
  422.7 5.0 gather_fusion.5
  427.7 5.0 gather_fusion.4
  432.7 5.0 gather_fusion.3
  437.7 5.0 gather_fusion.2
  442.6 4.0 fusion.12
  447.7 39.4 %reduce-scatter.2.cloned.1.call-done = bf16[128,256]{1,0:T(8,128)(2,1)} async-done(((bf16[128,2048]{1,0:T(8,128)(2,1)}), bf16[128,256]{1,0:T(8,128)(2,1)}) %reduce-scatter.2.cloned.1.call-update) | async-done | bytes 65552 | tf_op jit(solution)/shard_map/reduce_scatter | solution.py:152
  488.0 12.2 %all-gather = bf16[1,1,2048]{2,1,0:T(2,128)(2,1)S(1)} all-gather(bf16[1,1,256]{2,1,0:T(2,128)(2,1)S(1)} %slice.154), channel_id=2, replica_groups=mesh['req'=32,'tp'=8] {'tp'}, dimensions={2}, use_global_device_ids=true | all-gather | bytes 4608 | tf_op jit(solution)/shard_map/all_gather | solution.py:158
  500.2 101.9 %all-gather.1 = bf16[32,1,2048]{2,1,0:T(2,128)(2,1)S(1)} all-gather(bf16[1,1,2048]{2,1,0:T(2,128)(2,1)S(1)} %all-gather), channel_id=3, replica_groups=mesh['req'=32,'tp'=8] {'req'}, dimensions={0}, use_global_device_ids=true | all-gather | bytes 135168 | tf_op jit(solution)/shard_map/all_gather | solution.py:159
  604.8 84.9 %pmax.7 = f32[32]{0:T(128)} all-reduce(f32[32]{0:T(128)S(1)} %convolution_reduce_fusion), channel_id=1, replica_groups=mesh['req'=32,'tp'=8] {'req','tp'}, use_global_device_ids=true, to_apply=%region_15.17 | all-reduce | flops 32 | bytes 256 | tf_op jit(solution)/shard_map/pmax | solution.py:166
  (135 shorter events, 61.5 us)
Async XLA Ops:
  7.2 77.3 %copy-start = (bf16[3,2048,256]{2,1,0:T(8,128)(2,1)S(1)}, bf16[3,2048,256]{2,1,0:T(8,128)(2,1)}, u32[]{:S(2)}) copy-start(bf16[3,2048,256]{2,1,0:T(8,128)(2,1)} %param.20) | copy-start | bytes 9437188
  10.7 14.8 %copy-start.13 = (s32[128,6]{0,1:T(8,128)S(1)}, s32[128,6]{0,1:T(8,128)}, u32[]{:S(2)}) copy-start(s32[128,6]{0,1:T(8,128)} %param.27) | copy-start | bytes 9220
  10.7 15.9 %copy-start.15 = (bf16[2048]{0:T(1024)(128)(2,1)S(1)}, bf16[2048]{0:T(1024)(128)(2,1)}, u32[]{:S(2)}) copy-start(bf16[2048]{0:T(1024)(128)(2,1)} %param.19) | copy-start | bytes 12292
  10.7 15.9 %copy-start.16 = (bf16[2048]{0:T(1024)(128)(2,1)S(1)}, bf16[2048]{0:T(1024)(128)(2,1)}, u32[]{:S(2)}) copy-start(bf16[2048]{0:T(1024)(128)(2,1)} %param.25) | copy-start | bytes 12292
  10.7 19.0 %copy-start.20 = (s32[32]{0:T(128)S(1)}, s32[32]{0:T(128)}, u32[]{:S(2)}) copy-start(s32[32]{0:T(128)} %param.23) | copy-start | bytes 388
  10.7 35.8 %copy-start.11 = (bf16[128,256]{1,0:T(8,128)(2,1)S(1)}, bf16[128,256]{1,0:T(8,128)(2,1)}, u32[]{:S(2)}) copy-start(bf16[128,256]{1,0:T(8,128)(2,1)} %param.18) | copy-start | bytes 196612
  10.7 35.8 %all-to-all-start.1 = ((bf16[2,1,1024,256]{3,0,1,2:T(2,128)(2,1)}), bf16[2,1,1024,256]{3,0,1,2:T(2,128)(2,1)}, u32[]{:S(2)}, u32[]{:S(2)}) async-start(bf16[2,1,1024,256]{3,0,1,2:T(2,128)(2,1)} %copy.95), calls=%async_computation.1 | async-start | bytes 2097152 | tf_op jit(solution)/shard_map/all_to_all | solution.py:101
  47.3 28.6 %all-to-all-start = ((bf16[8,128,256]{2,1,0:T(8,128)(2,1)}), bf16[8,128,256]{2,1,0:T(8,128)(2,1)}, u32[]{:S(2)}, u32[]{:S(2)}) async-start(bf16[8,128,256]{2,1,0:T(8,128)(2,1)} %stack.4), calls=%async_computation | async-start | bytes 1048576 | tf_op jit(solution)/shard_map/all_to_all | solution.py:84
  76.0 31.7 %all-to-all-start.2 = ((bf16[2,32,32,256]{3,2,0,1:T(8,128)(2,1)}), bf16[2,32,32,256]{3,2,0,1:T(8,128)(2,1)}, u32[]{:S(2)}, u32[]{:S(2)}) async-start(bf16[2,32,32,256]{3,2,0,1:T(8,128)(2,1)} %select_bitcast_fusion), calls=%async_computation.2 | async-start | bytes 2097152 | tf_op jit(solution)/shard_map/all_to_all | solution.py:103
  80.6 111.3 %all-reduce.3.cloned.1.call-start = ((), (), s32[]{:S(2)}) async-start(), calls=%async_computation.6 | async-start | bytes 1048576 | tf_op jit(solution)/shard_map/psum | solution.py:108
  82.9 2.3 copy-start.1
  111.9 5.9 copy-start.7
  111.9 5.9 copy-start.10
  121.2 2.0 copy-start.6
  124.3 70.1 %copy-start.12 = (f32[2048]{0:T(1024)S(1)}, f32[2048]{0:T(1024)}, u32[]{:S(2)}) copy-start(f32[2048]{0:T(1024)} %convert_element_type.198) | copy-start | bytes 24580
  208.9 106.0 %copy-start.18 = (bf16[1,2,2048,176]{2,3,1,0:T(8,128)(2,1)S(1)}, bf16[1,2,2048,176]{2,3,1,0:T(8,128)(2,1)}, u32[]{:S(2)}) copy-start(bf16[1,2,2048,176]{2,3,1,0:T(8,128)(2,1)} %param.28) | copy-start | bytes 4325380
  314.9 2.3 copy-start.19
  320.6 7.4 %copy-start.8 = (bf16[2048,32]{0,1:T(8,128)(2,1)S(1)}, bf16[2048,32]{0,1:T(8,128)(2,1)}, u32[]{:S(2)}) copy-start(bf16[2048,32]{0,1:T(8,128)(2,1)} %param.26) | copy-start | bytes 393220
  320.6 8.8 %copy-start.14 = (s32[128,6]{0,1:T(8,128)S(1)}, s32[128,6]{0,1:T(8,128)}, u32[]{:S(2)}) copy-start(s32[128,6]{0,1:T(8,128)} %param.27) | copy-start | bytes 9220
  320.6 92.2 %all-to-all-start.4 = ((bf16[32,1,32,2048]{3,2,1,0:T(8,128)(2,1)}), bf16[32,1,32,2048]{3,2,1,0:T(8,128)(2,1)}, u32[]{:S(2)}, u32[]{:S(2)}) async-start(bf16[32,1,32,2048]{3,2,1,0:T(8,128)(2,1)} %convert_bitcast_fusion), calls=%async_computation.4 | async-start | bytes 8388608 | tf_op jit(solution)/shard_map/all_to_all | solution.py:146
  327.5 159.6 %reduce-scatter.2.cloned.1.call-start = ((), (), s32[]{:S(2)}) async-start(), calls=%async_computation.7 | async-start | bytes 589824 | tf_op jit(solution)/shard_map/reduce_scatter | solution.py:152
  442.6 4.1 copy-start.17
  488.0 116.8 %copy-start.9 = (bf16[128,256]{1,0:T(8,128)(2,1)}, bf16[128,256]{1,0:T(8,128)(2,1)S(1)}, u32[]{:S(2)}) copy-start(bf16[128,256]{1,0:T(8,128)(2,1)S(1)} %add_convert_fusion.1) | copy-start | bytes 196612
  602.5 87.3 %copy-start.21 = (f32[32]{0:T(128)}, f32[32]{0:T(128)S(1)}, u32[]{:S(2)}) copy-start(f32[32]{0:T(128)S(1)} %add_sqrt_fusion) | copy-start | bytes 388
  (4 other events, 4.4 us)
Sparse Core Ops, SparseCore 0:
  124.5 67.4 all-reduce.2
  446.8 40.2 reduce-scatter.1
